TPU v7x, 512 devices: a whole 4x4x16 slice. The times are simulated.
512 devices in a mesh: sector: 16 (over y, x_lo, core), dom: 32 (over z, x_hi).
Axes of the slice: x: 4 (x_hi: 2, x_lo: 2; x = x_hi * 2 + x_lo), y: 4, z: 16, core: 2. Of those that a mesh axis runs over, the one named last changes fastest.
Arguments:
- amplitudes: float32 [64, 48], replicated, may hold values from -0.3 to 0.3
- mode_shapes: float32 [48, 3, 524288], P(None, None, ('sector', 'dom')), may hold values from -6 to 6
- shape_grads: float32 [8, 3, 524288], P(None, None, ('sector', 'dom')), may hold values from -2.4 to 2.4
- lame_params: float32 [2, 524288], P(None, ('sector', 'dom')), may hold values from 0.5 to 2
- connectivity: int32 [8, 524288], P(None, ('sector', 'dom')), may hold values from -1 to 1791, as said below
- dom_sends: int32 [2, 131072], P(None, ('sector', 'dom')), may hold values from -1 to 1023, as said below
- sector_sends: int32 [2, 65536], P(None, ('sector', 'dom')), may hold values from -1 to 1023, as said below
Outputs:
- nodal_force: float32 [64, 3, 524288], P(None, None, ('sector', 'dom'))
- modal_force: float32 [64, 48], replicated
Inputs may be any that keep to these rules, and one draw needn't show every extreme that they name: `connectivity`: in each device's block, the live elements come first and the padding element slots after them hold -1 in all 8 rows; a live slot names a slot of the device's extended table. Some device has all 1024 slots live. `dom_sends`: each device's row lists its own node numbers first, then -1; a row holds 128 to 256 live entries, and some row is full. `sector_sends`: each device's row lists its own node numbers first, then -1; a row holds 64 to 128 live entries, and some row is full.
All inputs are finite; a program needn't handle non-finite values.
Results may differ from a plain program's by a relative error of at most 0.0003.
Values sent between devices are 32-bit elements; how exact they have to be, the bound alone decides.
A program may use at most 64 MiB of HBM per device.

v0:
```python
import math
import jax
import jax.numpy as jnp
from jax import lax
from jax.sharding import PartitionSpec as P


def padded(cells, sides, width, closed):
    for axis, dim in sides:
        count = lax.axis_size(axis)
        ends = count if closed else count - 1
        head = lax.slice_in_dim(cells, 0, width, axis=dim)
        tail = lax.slice_in_dim(cells, cells.shape[dim] - width, cells.shape[dim], axis=dim)
        cells = jnp.concatenate(
            [
                lax.ppermute(tail, axis, [(i, (i + 1) % count) for i in range(ends)]),
                cells,
                lax.ppermute(head, axis, [((i + 1) % count, i) for i in range(ends)]),
            ],
            axis=dim,
        )
    return cells


def take_slots(node_table, send_lists):
    slot_width = node_table.shape[1]
    slot_index = jnp.where(send_lists < 0, slot_width, send_lists).reshape(-1)
    return jnp.take(node_table, slot_index, axis=1, mode="fill", fill_value=0.0)


def add_slots(node_table, send_lists, add_values):
    slot_width = node_table.shape[1]
    slot_index = jnp.where(send_lists < 0, slot_width, send_lists).reshape(-1)
    return node_table.at[:, slot_index].add(add_values, mode="drop")


def element_forces(accum, extended, connect, gradients, lame):
    ext_width = extended.shape[1]
    combo_total = extended.shape[0] // 3
    elem_total = connect.shape[1]
    slot_index = jnp.where(connect < 0, ext_width, connect).reshape(-1)
    corners = jnp.take(extended, slot_index, axis=1, mode="fill", fill_value=0.0).reshape(
        combo_total, 3, 8, elem_total
    )
    gradient = jnp.zeros((combo_total, 3, 3, elem_total), extended.dtype)
    for corner in range(8):
        gradient = gradient + corners[:, :, None, corner, :] * gradients[corner][None, None, :, :]
    quadratic = jnp.sum(gradient[:, :, :, None, :] * gradient[:, :, None, :, :], axis=1)
    green_strain = 0.5 * (gradient + jnp.swapaxes(gradient, 1, 2) + quadratic)
    strain_trace = green_strain[:, 0, 0] + green_strain[:, 1, 1] + green_strain[:, 2, 2]
    identity = jnp.eye(3, dtype=extended.dtype)[None, :, :, None]
    stress = lame[0] * strain_trace[:, None, None, :] * identity + 2.0 * lame[1] * green_strain
    piola = stress + jnp.sum(gradient[:, :, :, None, :] * stress[:, None, :, :, :], axis=2)
    corner_forces = jnp.stack(
        [jnp.sum(piola * gradients[corner][None, None, :, :], axis=2) for corner in range(8)],
        axis=2,
    )
    return accum.at[:, slot_index].add(
        corner_forces.reshape(3 * combo_total, 8 * elem_total), mode="drop"
    )


def outer_ends(ext_rows, slot_width):
    return jnp.concatenate([ext_rows[:, :slot_width], ext_rows[:, 3 * slot_width :]], axis=1)


def local(amplitudes, mode_shapes, shape_grads, lame_params, connectivity, dom_sends, sector_sends):
    modes_total, _, node_total = mode_shapes.shape
    combo_total = amplitudes.shape[0]
    table_rows = 3 * combo_total
    dom_width = dom_sends.shape[1]
    sec_width = sector_sends.shape[1]
    flat_shapes = mode_shapes.reshape(modes_total, 3 * node_total)
    displaced = jnp.dot(
        amplitudes, flat_shapes, precision=lax.Precision.HIGHEST, preferred_element_type=jnp.float32
    ).reshape(table_rows, node_total)
    dom_ext = padded(take_slots(displaced, dom_sends), (("dom", 1),), dom_width, False)
    sec_ext = padded(take_slots(displaced, sector_sends), (("sector", 1),), sec_width, True)
    halo_moved = jnp.concatenate(
        [outer_ends(dom_ext, dom_width), outer_ends(sec_ext, sec_width)], axis=1
    )
    extended = jnp.concatenate([displaced, halo_moved], axis=1)
    ext_width = extended.shape[1]
    elem_total = connectivity.shape[1]
    block_size = math.gcd(elem_total, 256)
    turn_total = elem_total // block_size

    def one_block(turn_index, forces):
        first_col = turn_index * block_size
        connect_block = lax.dynamic_slice_in_dim(connectivity, first_col, block_size, 1)
        grads_block = lax.dynamic_slice_in_dim(shape_grads, first_col, block_size, 2)
        lame_block = lax.dynamic_slice_in_dim(lame_params, first_col, block_size, 1)
        return element_forces(forces, extended, connect_block, grads_block, lame_block)

    slot_forces = lax.fori_loop(
        0, turn_total, one_block, jnp.zeros((table_rows, ext_width), jnp.float32)
    )
    own_forces = slot_forces[:, :node_total]
    dom_back = slot_forces[:, node_total : node_total + 2 * dom_width]
    sec_back = slot_forces[:, node_total + 2 * dom_width :]
    dom_return = padded(dom_back, (("dom", 1),), dom_width, False)
    own_forces = add_slots(own_forces, dom_sends, outer_ends(dom_return, dom_width))
    sec_return = padded(sec_back, (("sector", 1),), sec_width, True)
    own_forces = add_slots(own_forces, sector_sends, outer_ends(sec_return, sec_width))
    partial_modal = lax.dot_general(
        own_forces.reshape(combo_total, 3 * node_total),
        flat_shapes,
        (((1,), (1,)), ((), ())),
        precision=lax.Precision.HIGHEST,
        preferred_element_type=jnp.float32,
    )
    modal_total = lax.psum(partial_modal, ("sector", "dom"))
    all_nodes = node_total * lax.axis_size("sector") * lax.axis_size("dom")
    return (
        own_forces.reshape(combo_total, 3, node_total),
        modal_total / math.sqrt(3.0 * all_nodes),
    )


def solution(mesh):
    placed = (
        P(),
        P(None, None, ("sector", "dom")),
        P(None, None, ("sector", "dom")),
        P(None, ("sector", "dom")),
        P(None, ("sector", "dom")),
        P(None, ("sector", "dom")),
        P(None, ("sector", "dom")),
    )
    return jax.shard_map(
        local,
        mesh=mesh,
        in_specs=placed,
        out_specs=(P(None, None, ("sector", "dom")), P()),
        check_vma=False,
    )
```

profile of v0, /device:TPU:1, one launch (start us, length us, event | category | flops | bytes accessed | tf_op | source)
XLA Modules:
  0.0 308.0 jit_solution(2652404135059010113)
XLA Ops:
  7.1 5.5 %collective-permute-start = (f32[192,256]{0,1:T(8,128)S(1)}, f32[192,256]{0,1:T(8,128)S(1)}, u32[]{:S(2)}, u32[]{:S(2)}) collective-permute-start(f32[192,256]{0,1:T(8,128)S(1)} %get-tuple-element.244), channel_id=1, source_target_pairs={{0,1},{1,2},{2,3},{3,4},{4,5},{5,6},{6,7},{7,8},{8,9},{9,10},{10,1... | collective-permute-start | bytes 589832 | tf_op jit(solution)/shard_map/ppermute | solution.py:16
  13.7 4.6 %collective-permute-start.3 = (f32[192,128]{0,1:T(8,128)S(1)}, f32[192,128]{0,1:T(8,128)S(1)}, u32[]{:S(2)}, u32[]{:S(2)}) collective-permute-start(f32[192,128]{0,1:T(8,128)S(1)} %get-tuple-element.245), channel_id=1, source_target_pairs={{32,0},{64,32},{96,64},{128,96},{160,128},{192,160},{224,192},{256... | collective-permute-start | bytes 294920 | tf_op jit(solution)/shard_map/ppermute | solution.py:18
  18.4 1.9 collective-permute-start.2
  21.9 9.2 %collective-permute-done.1 = f32[192,256]{0,1:T(8,128)S(1)} collective-permute-done((f32[192,256]{0,1:T(8,128)S(1)}, f32[192,256]{0,1:T(8,128)S(1)}, u32[]{:S(2)}, u32[]{:S(2)}) %collective-permute-start.1) | collective-permute-done | bytes 196640 | tf_op jit(solution)/shard_map/ppermute | solution.py:18
  32.4 136.4 %while.15 = (s32[]{:T(128)}, f32[192,1792]{0,1:T(8,128)S(1)}, s32[8,1024]{1,0:T(8,128)S(1)}, f32[2,1024]{1,0:T(2,128)}, f32[192,1792]{0,1:T(8,128)}, /*index=5*/...) while((s32[]{:T(128)}, f32[192,1792]{0,1:T(8,128)S(1)}, ...), condition=%wide.region_12.13_spmd, body=%wide.region_0.12_spmd.sunk | while | flops 12415007 | bytes 49229240 | solution.py:95
  34.6 10.1 %gather_fusion = f32[2048,192]{1,0:T(8,128)} fusion(f32[192,1792]{0,1:T(8,128)} %get-tuple-element.414, s32[2048]{0:T(1024)S(1)} %broadcast_clamp_fusion.2), kind=kCustom, calls=%fused_computation.clone.1 | custom fusion | bytes 3153920 | tf_op jit(solution)/shard_map/while/body/eval_jaxpr/jit(_take)/gather | solution.py:42
  44.7 1.9 copy.147
  53.8 12.6 %scatter_fusion = f32[192,1792]{0,1:T(8,128)S(1)} fusion(f32[192,1792]{0,1:T(8,128)S(1)} %get-tuple-element.394, s32[2048]{0:T(1024)S(1)} %bitcast.158, f32[2048,192]{1,0:T(8,128)} %copy.151), kind=kCustom, calls=%fused_computation.3.clone.1 | custom fusion | flops 393216 | bytes 4726784 | tf_op jit(solution)/shard_map/while/body/eval_jaxpr/scatter-add | solution.py:58
  68.8 10.1 %gather_fusion = f32[2048,192]{1,0:T(8,128)} fusion(f32[192,1792]{0,1:T(8,128)} %get-tuple-element.414, s32[2048]{0:T(1024)S(1)} %broadcast_clamp_fusion.2), kind=kCustom, calls=%fused_computation.clone.1 | custom fusion | bytes 3153920 | tf_op jit(solution)/shard_map/while/body/eval_jaxpr/jit(_take)/gather | solution.py:42
  78.8 1.9 copy.147
  87.9 12.6 %scatter_fusion = f32[192,1792]{0,1:T(8,128)S(1)} fusion(f32[192,1792]{0,1:T(8,128)S(1)} %get-tuple-element.394, s32[2048]{0:T(1024)S(1)} %bitcast.158, f32[2048,192]{1,0:T(8,128)} %copy.151), kind=kCustom, calls=%fused_computation.3.clone.1 | custom fusion | flops 393216 | bytes 4726784 | tf_op jit(solution)/shard_map/while/body/eval_jaxpr/scatter-add | solution.py:58
  102.8 10.1 %gather_fusion = f32[2048,192]{1,0:T(8,128)} fusion(f32[192,1792]{0,1:T(8,128)} %get-tuple-element.414, s32[2048]{0:T(1024)S(1)} %broadcast_clamp_fusion.2), kind=kCustom, calls=%fused_computation.clone.1 | custom fusion | bytes 3153920 | tf_op jit(solution)/shard_map/while/body/eval_jaxpr/jit(_take)/gather | solution.py:42
  112.9 1.9 copy.147
  122.0 12.6 %scatter_fusion = f32[192,1792]{0,1:T(8,128)S(1)} fusion(f32[192,1792]{0,1:T(8,128)S(1)} %get-tuple-element.394, s32[2048]{0:T(1024)S(1)} %bitcast.158, f32[2048,192]{1,0:T(8,128)} %copy.151), kind=kCustom, calls=%fused_computation.3.clone.1 | custom fusion | flops 393216 | bytes 4726784 | tf_op jit(solution)/shard_map/while/body/eval_jaxpr/scatter-add | solution.py:58
  137.0 10.1 %gather_fusion = f32[2048,192]{1,0:T(8,128)} fusion(f32[192,1792]{0,1:T(8,128)} %get-tuple-element.414, s32[2048]{0:T(1024)S(1)} %broadcast_clamp_fusion.2), kind=kCustom, calls=%fused_computation.clone.1 | custom fusion | bytes 3153920 | tf_op jit(solution)/shard_map/while/body/eval_jaxpr/jit(_take)/gather | solution.py:42
  147.0 1.9 copy.147
  156.1 12.6 %scatter_fusion = f32[192,1792]{0,1:T(8,128)S(1)} fusion(f32[192,1792]{0,1:T(8,128)S(1)} %get-tuple-element.394, s32[2048]{0:T(1024)S(1)} %bitcast.158, f32[2048,192]{1,0:T(8,128)} %copy.151), kind=kCustom, calls=%fused_computation.3.clone.1 | custom fusion | flops 393216 | bytes 4726784 | tf_op jit(solution)/shard_map/while/body/eval_jaxpr/scatter-add | solution.py:58
  168.8 2.8 collective-permute-start.4
  173.6 4.8 %collective-permute-start.6 = (f32[192,128]{0,1:T(8,128)}, f32[192,128]{0,1:T(8,128)}, u32[]{:S(2)}, u32[]{:S(2)}) collective-permute-start(f32[192,128]{0,1:T(8,128)} %get-tuple-element.239), channel_id=1, source_target_pairs={{0,32},{32,64},{64,96},{96,128},{128,160},{160,192},{192,224},{224... | collective-permute-start | bytes 294920 | tf_op jit(solution)/shard_map/ppermute | solution.py:16
  178.4 2.2 collective-permute-start.7
  180.7 3.8 %scatter_custom_fusion.1 = f32[192,1024]{0,1:T(8,128)S(1)} fusion(f32[192,1024]{0,1:T(8,128)S(1)} %slice.257, s32[512]{0:T(512)S(1)} %bitcast.167, f32[192,256]{0,1:T(8,128)S(1)} %collective-permute-done.5, f32[]{:T(128)} %constant.154, f32[192,256]{0,1:T(8,128)S(1)} %collective-permute-done.4), kind=kCustom, calls=%fused_computation.67 | custom fusion | flops 196608 | bytes 1310724 | tf_op jit(solution)/shard_map/scatter-add | solution.py:34
  185.4 4.3 %collective-permute-done.7 = f32[192,128]{0,1:T(8,128)} collective-permute-done((f32[192,128]{0,1:T(8,128)}, f32[192,128]{0,1:T(8,128)}, u32[]{:S(2)}, u32[]{:S(2)}) %collective-permute-start.7) | collective-permute-done | bytes 98336 | tf_op jit(solution)/shard_map/ppermute | solution.py:18
  189.6 3.0 scatter_custom_fusion.2
  194.8 111.2 %psum.7 = f32[64,48]{0,1:T(8,128)S(1)} all-reduce(f32[64,48]{0,1:T(8,128)S(1)} %fusion.18), channel_id=1, replica_groups=mesh['sector'=16,'dom'=32] {'sector','dom'}, use_global_device_ids=true, to_apply=%region_15.16 | all-reduce | flops 3072 | bytes 24576 | tf_op jit(solution)/shard_map/psum | solution.py:112
  (202 shorter events, 54.3 us)
Async XLA Ops:
  0.6 3.4 %copy-start = (f32[64,48]{0,1:T(8,128)S(1)}, f32[64,48]{0,1:T(8,128)}, u32[]{:S(2)}) copy-start(f32[64,48]{0,1:T(8,128)} %param.9) | copy-start | bytes 36868
  3.2 0.8 copy-start.2
  6.9 5.7 %copy-start.5 = (s32[2,128]{1,0:T(2,128)S(1)}, s32[2,128]{1,0:T(2,128)}, u32[]{:S(2)}) copy-start(s32[2,128]{1,0:T(2,128)} %param.15) | copy-start | bytes 3076
  7.1 14.8 %collective-permute-start = (f32[192,256]{0,1:T(8,128)S(1)}, f32[192,256]{0,1:T(8,128)S(1)}, u32[]{:S(2)}, u32[]{:S(2)}) collective-permute-start(f32[192,256]{0,1:T(8,128)S(1)} %get-tuple-element.244), channel_id=1, source_target_pairs={{0,1},{1,2},{2,3},{3,4},{4,5},{5,6},{6,7},{7,8},{8,9},{9,10},{10,1... | collective-permute-start | bytes 589832 | tf_op jit(solution)/shard_map/ppermute | solution.py:16
  13.7 17.4 %collective-permute-start.3 = (f32[192,128]{0,1:T(8,128)S(1)}, f32[192,128]{0,1:T(8,128)S(1)}, u32[]{:S(2)}, u32[]{:S(2)}) collective-permute-start(f32[192,128]{0,1:T(8,128)S(1)} %get-tuple-element.245), channel_id=1, source_target_pairs={{32,0},{64,32},{96,64},{128,96},{160,128},{192,160},{224,192},{256... | collective-permute-start | bytes 294920 | tf_op jit(solution)/shard_map/ppermute | solution.py:18
  18.4 12.7 %collective-permute-start.2 = (f32[192,128]{0,1:T(8,128)S(1)}, f32[192,128]{0,1:T(8,128)S(1)}, u32[]{:S(2)}, u32[]{:S(2)}) collective-permute-start(f32[192,128]{0,1:T(8,128)S(1)} %get-tuple-element.246), channel_id=1, source_target_pairs={{0,32},{32,64},{64,96},{96,128},{128,160},{160,192},{192,224},{224... | collective-permute-start | bytes 294920 | tf_op jit(solution)/shard_map/ppermute | solution.py:16
  20.3 10.8 %collective-permute-start.1 = (f32[192,256]{0,1:T(8,128)S(1)}, f32[192,256]{0,1:T(8,128)S(1)}, u32[]{:S(2)}, u32[]{:S(2)}) collective-permute-start(f32[192,256]{0,1:T(8,128)S(1)} %get-tuple-element.243), channel_id=1, source_target_pairs={{1,0},{2,1},{3,2},{4,3},{5,4},{6,5},{7,6},{8,7},{9,8},{10,9},{11,1... | collective-permute-start | bytes 589832 | tf_op jit(solution)/shard_map/ppermute | solution.py:18
  21.9 10.5 %copy-start.4 = (s32[8,1024]{1,0:T(8,128)S(1)}, s32[8,1024]{1,0:T(8,128)}, u32[]{:S(2)}) copy-start(s32[8,1024]{1,0:T(8,128)} %param.13) | copy-start | bytes 98308
  31.1 1.2 copy-start.1
  168.8 11.9 %collective-permute-start.4 = (f32[192,256]{0,1:T(8,128)S(1)}, f32[192,256]{0,1:T(8,128)S(1)}, u32[]{:S(2)}, u32[]{:S(2)}) collective-permute-start(f32[192,256]{0,1:T(8,128)S(1)} %get-tuple-element.241), channel_id=1, source_target_pairs={{0,1},{1,2},{2,3},{3,4},{4,5},{5,6},{6,7},{7,8},{8,9},{9,10},{10,1... | collective-permute-start | bytes 589832 | tf_op jit(solution)/shard_map/ppermute | solution.py:16
  171.6 9.1 %collective-permute-start.5 = (f32[192,256]{0,1:T(8,128)S(1)}, f32[192,256]{0,1:T(8,128)S(1)}, u32[]{:S(2)}, u32[]{:S(2)}) collective-permute-start(f32[192,256]{0,1:T(8,128)S(1)} %get-tuple-element.242), channel_id=1, source_target_pairs={{1,0},{2,1},{3,2},{4,3},{5,4},{6,5},{7,6},{8,7},{9,8},{10,9},{11,1... | collective-permute-start | bytes 589832 | tf_op jit(solution)/shard_map/ppermute | solution.py:18
  173.6 11.8 %collective-permute-start.6 = (f32[192,128]{0,1:T(8,128)}, f32[192,128]{0,1:T(8,128)}, u32[]{:S(2)}, u32[]{:S(2)}) collective-permute-start(f32[192,128]{0,1:T(8,128)} %get-tuple-element.239), channel_id=1, source_target_pairs={{0,32},{32,64},{64,96},{96,128},{128,160},{160,192},{192,224},{224... | collective-permute-start | bytes 294920 | tf_op jit(solution)/shard_map/ppermute | solution.py:16
  178.4 11.3 %collective-permute-start.7 = (f32[192,128]{0,1:T(8,128)}, f32[192,128]{0,1:T(8,128)}, u32[]{:S(2)}, u32[]{:S(2)}) collective-permute-start(f32[192,128]{0,1:T(8,128)} %get-tuple-element.240), channel_id=1, source_target_pairs={{32,0},{64,32},{96,64},{128,96},{160,128},{192,160},{224,192},{256... | collective-permute-start | bytes 294920 | tf_op jit(solution)/shard_map/ppermute | solution.py:18
  193.0 1.1 copy-start.3
where the time goes:
time: 309 us; the launch traced here: 308 us
  blocking collectives  111 us (36%)
  local copies, waits for them, and re-layouts  87.5 us (28%)
  other arithmetic  66.7 us (22%)
  starting transfers between devices  24.6 us (8%)
  waiting for transfers between devices  14.3 us (5%)
    psum x1, blocking collectives, local(): modal_total = lax.psum(partial_modal, ('sector', 'dom'))  111 us
    scatter-add x4, other arithmetic, element_forces(): accum.at[:, slot_index]  50.6 us
    gather x8, local copies, waits for them, and re-layouts, element_forces(): jnp.take(extended, slot_index, axis=1, mode='fill', fill_value=0.0)  47.8 us
    ppermute x4, starting transfers between devices, padded(): lax.ppermute(tail, axis, [(i, (i + 1) % count) for i in range(ends)])  15 us
    ppermute x4, waiting for transfers between devices, padded(): lax.ppermute(head, axis, [((i + 1) % count, i) for i in range(ends)])  13.4 us
    ppermute x4, starting transfers between devices, padded(): lax.ppermute(head, axis, [((i + 1) % count, i) for i in range(ends)])  9.62 us
    reshape x4, local copies, waits for them, and re-layouts, element_forces(): corner_forces.reshape(3 * combo_total, 8 * elem_total)  7.39 us
    scatter-add x2, other arithmetic, add_slots(): return node_table.at[:, slot_index].add(add_values, mode='drop')  6.78 us
  transfers between devices with their start and end apart: 8, of which 3 were waited for; matrix products, arithmetic and copies ran while one was open for 2% of the time, Pallas kernels for 0%

commit v1 on v0

--- a/solution.py
+++ b/solution.py
@@ -109,7 +109,7 @@
         precision=lax.Precision.HIGHEST,
         preferred_element_type=jnp.float32,
     )
-    modal_total = lax.psum(partial_modal, ("sector", "dom"))
+    modal_total = jnp.sum(lax.all_gather(partial_modal, ("sector", "dom")), axis=0)
     all_nodes = node_total * lax.axis_size("sector") * lax.axis_size("dom")
     return (
         own_forces.reshape(combo_total, 3, node_total),

time: 309 us -> 1650 us (5.34)
  waiting for transfers between devices: 14.3 us -> 1450 us
  blocking collectives: 111 us -> 0 us
    all_gather x0 -> x1, waiting for transfers between devices: none -> 1430 us  [local(): lax.all_gather(partial_modal, ('sector', 'dom'))]
    psum x1 -> x0, blocking collectives: 111 us -> none  [local(): modal_total = lax.psum(partial_modal, ('sector', 'dom'))]
  transfers between devices with their start and end apart: 8 -> 9, of which waited for: 3 -> 4; matrix products, arithmetic and copies ran while one was open for 2% -> 1% of each run, Pallas kernels for 0% -> 0%
where the time goes in v1:
time: 1650 us
  waiting for transfers between devices  1450 us (88%)
  local copies, waits for them, and re-layouts  89.2 us (5%)
  other arithmetic  72.2 us (4%)
  starting transfers between devices  24.6 us (1%)
    all_gather x1, waiting for transfers between devices, local(): lax.all_gather(partial_modal, ('sector', 'dom'))  1430 us
    scatter-add x4, other arithmetic, element_forces(): accum.at[:, slot_index]  50.6 us
    gather x8, local copies, waits for them, and re-layouts, element_forces(): jnp.take(extended, slot_index, axis=1, mode='fill', fill_value=0.0)  47.8 us
  transfers between devices with their start and end apart: 9, of which 4 were waited for; matrix products, arithmetic and copies ran while one was open for 1% of the time, Pallas kernels for 0%

profile of v1, /device:TPU:1, one launch (start us, length us, event | category | flops | bytes accessed | tf_op | source)
XLA Modules:
  0.0 1649.3 jit_solution(5571730572772006597)
XLA Ops:
  12.9 5.5 collective-permute-start
  19.5 4.6 collective-permute-start.3
  24.2 1.9 collective-permute-start.2
  29.4 7.5 collective-permute-done.1
  39.0 136.3 %while.15 = (s32[]{:T(128)}, f32[192,1792]{0,1:T(8,128)S(1)}, s32[8,1024]{1,0:T(8,128)S(1)}, f32[2,1024]{1,0:T(2,128)}, f32[192,1792]{0,1:T(8,128)}, /*index=5*/...) while((s32[]{:T(128)}, f32[192,1792]{0,1:T(8,128)S(1)}, ...), condition=%wide.region_12.13_spmd, body=%wide.region_0.12_spmd.sunk | while | flops 12415007 | bytes 49229240 | solution.py:95
  41.4 10.1 gather_fusion
  51.4 1.9 copy.182
  60.5 12.6 scatter_fusion
  75.5 10.1 gather_fusion
  85.5 1.9 copy.182
  94.6 12.6 scatter_fusion
  109.6 10.1 gather_fusion
  119.7 1.9 copy.182
  128.7 12.6 scatter_fusion
  143.5 10.1 gather_fusion
  162.7 12.6 scatter_fusion
  175.4 2.8 collective-permute-start.4
  180.2 4.8 collective-permute-start.6
  185.0 2.2 collective-permute-start.7
  187.3 3.8 scatter_custom_fusion.1
  192.0 4.3 collective-permute-done.7
  196.2 3.0 scatter_custom_fusion.2
  203.4 1433.0 %all-gather.4.cloned.1.call-done = f32[512,64,48]{1,2,0:T(8,128)} async-done(((f32[1,64,48]{1,2,0:T(8,128)}), f32[512,64,48]{1,2,0:T(8,128)}) %all-gather.4.cloned.1.call-update) | async-done | bytes 6291472 | tf_op jit(solution)/shard_map/all_gather | solution.py:112
  1636.4 5.5 reduce_sum.169
  (203 shorter events, 58.6 us)
Async XLA Ops:
  7.2 2.6 copy-start
  7.2 1629.2 %all-gather.4.cloned.1.call-start = ((), (), s32[]{:S(2)}) async-start(), calls=%async_computation | async-start | bytes 12607488 | tf_op jit(solution)/shard_map/all_gather | solution.py:112
  9.8 0.8 copy-start.1
  12.7 5.7 copy-start.4
  12.9 15.7 collective-permute-start
  19.5 18.7 %collective-permute-start.3 = (f32[192,128]{0,1:T(8,128)S(1)}, f32[192,128]{0,1:T(8,128)S(1)}, u32[]{:S(2)}, u32[]{:S(2)}) collective-permute-start(f32[192,128]{0,1:T(8,128)S(1)} %get-tuple-element.253), channel_id=1, source_target_pairs={{32,0},{64,32},{96,64},{128,96},{160,128},{192,160},{224,192},{256... | collective-permute-start | bytes 294920 | tf_op jit(solution)/shard_map/ppermute | solution.py:18
  24.2 13.4 collective-permute-start.2
  26.1 10.8 collective-permute-start.1
  28.6 10.4 copy-start.3
  175.4 11.9 collective-permute-start.4
  178.2 9.1 collective-permute-start.5
  180.2 11.8 collective-permute-start.6
  185.0 11.3 collective-permute-start.7
  199.2 1.1 copy-start.2
Sparse Core Ops, SparseCore 0:
  201.8 1434.4 all-gather.3
